TPU v7x, 256 devices: a whole 4x4x8 slice. The times are simulated.
256 devices in a mesh: patch: 32 (over y, z), req: 4 (over x), owner: 2 (over core).
Axes of the slice: x: 4, y: 4, z: 8, core: 2. Of those that a mesh axis runs over, the one named last changes fastest.
Arguments:
- latents: bfloat16 [8, 256, 256, 320], P('req', 'patch', 'owner'), may hold values from -24 to 24
- timestep_embedding: bfloat16 [8, 1280], P('req'), may hold values from -6 to 6
- embedding_weight: bfloat16 [1280, 320], replicated, may hold values from -0.15625 to 0.15625
- group_norm_gain: float32 [2, 320], replicated, may hold values from 0.25 to 1.75
- group_norm_shift: float32 [2, 320], replicated, may hold values from -3 to 3
- kernel_weight: bfloat16 [2, 9, 320, 320], replicated, may hold values from -0.109375 to 0.109375
- plugin_reduce_library: bfloat16 [8, 2, 184320], P(('req', 'owner'), None, 'patch'), may hold values from -0.109375 to 0.109375
- plugin_expand_library: bfloat16 [8, 2, 20480], P(('req', 'owner'), None, 'patch'), may hold values from -0.75 to 0.75
- image_adapter: int32 [8, 1], P('req'), may hold values from 0 to 7
- adapter_bank_row: int32 [8], replicated, may hold values from 0 to 7, each once
Outputs:
- result: bfloat16 [8, 256, 256, 320], P('req', 'patch', 'owner')
Inputs may be any that keep to these rules, and one draw needn't show every extreme that they name: `image_adapter`: each image names one adapter; every adapter is named by some image. A permutation: adapter a is stored in bank row adapter_bank_row[a].
All inputs are finite; a program needn't handle non-finite values.
Results may differ from a plain program's by a relative error of at most 0.0055.
Values may be sent and summed in bfloat16 or wider, within the bound.
A program may use at most 128 MiB of HBM per device.

v0:
```python
import jax
import jax.numpy as jnp
from jax import lax
from jax.sharding import PartitionSpec as P

GROUPS = 32


def padded_2(block, sides, width):
    for axis, dim in sides:
        count = lax.axis_size(axis)
        forward = [(i, i + 1) for i in range(count - 1)]
        backward = [(target, source) for source, target in forward]
        low = lax.ppermute(
            lax.slice_in_dim(block, block.shape[dim] - width, None, axis=dim), axis, forward
        )
        high = lax.ppermute(lax.slice_in_dim(block, 0, width, axis=dim), axis, backward)
        block = jnp.concatenate([low, block, high], axis=dim)
    return block


def group_act(values, gain, shift):
    images, rows, columns, chans = values.shape
    grouped = values.reshape(images, rows, columns, GROUPS, chans // GROUPS)
    count = rows * columns * (chans // GROUPS) * lax.axis_size("patch") * lax.axis_size("owner")
    total = lax.psum(jnp.sum(grouped, axis=(1, 2, 4)), ("patch", "owner"))
    mean = total / count
    centered = grouped - mean[:, None, None, :, None]
    spread = lax.psum(jnp.sum(centered * centered, axis=(1, 2, 4)), ("patch", "owner"))
    var = spread / count
    normed = (centered / jnp.sqrt(var + 1e-05)[:, None, None, :, None]).reshape(values.shape)
    return jax.nn.silu(normed * gain + shift).astype(jnp.bfloat16)


def block_conv(act, kernel, reducing_filter, expanding_linear_map):
    images, rows, columns, chans = act.shape
    outward = kernel.shape[2]
    padded = padded_2(act, (("patch", 1), ("owner", 2)), 1)
    joined = jnp.concatenate(
        [jnp.broadcast_to(kernel[None], (images,) + kernel.shape), reducing_filter], axis=3
    )
    accum = jnp.zeros((images, rows, columns, joined.shape[3]), jnp.float32)
    for tap in range(9):
        row_off, col_off = divmod(tap, 3)
        window = padded[:, row_off : row_off + rows, col_off : col_off + columns, :]
        accum = accum + jnp.einsum(
            "bhwc,bcd->bhwd", window, joined[:, tap], preferred_element_type=jnp.float32
        )
    lowpart = accum[..., outward:].astype(jnp.bfloat16)
    return accum[..., :outward] + jnp.einsum(
        "bhwr,brd->bhwd", lowpart, expanding_linear_map, preferred_element_type=jnp.float32
    )


def local(
    latents,
    timestep_embedding,
    embedding_weight,
    group_norm_gain,
    group_norm_shift,
    kernel_weight,
    plugin_reduce_library,
    plugin_expand_library,
    image_adapter,
    adapter_bank_row,
):
    images, rows, columns, chans = latents.shape
    wanted = image_adapter[:, 0]
    table = jnp.arange(adapter_bank_row.shape[0], dtype=jnp.int32)
    slots = jnp.sum(
        jnp.where(wanted[:, None] == table[None, :], adapter_bank_row[None, :], 0), axis=1
    )
    full_down, full_up = (
        lax.all_gather(plugin_reduce_library, "patch", axis=2, tiled=True),
        lax.all_gather(plugin_expand_library, "patch", axis=2, tiled=True),
    )
    pieces = (
        lax.all_gather(full_down, ("req", "owner"), axis=0, tiled=True),
        lax.all_gather(full_up, ("req", "owner"), axis=0, tiled=True),
    )
    count = pieces[0].shape[0]
    match = (slots[:, None] == jnp.arange(count, dtype=jnp.int32)[None, :]).astype(jnp.bfloat16)
    first = jnp.einsum("ik,kjs->ijs", match, pieces[0], preferred_element_type=jnp.float32)
    second = jnp.einsum("ik,kjs->ijs", match, pieces[1], preferred_element_type=jnp.float32)
    down_sel = first.astype(jnp.bfloat16)
    up_sel = second.astype(jnp.bfloat16)
    rank = up_sel.shape[2] // chans
    down_all = down_sel.reshape(images, 2, 9, chans, rank)
    up_all = up_sel.reshape(images, 2, rank, chans)
    temb = jax.nn.silu(timestep_embedding.astype(jnp.float32)).astype(jnp.bfloat16)
    proj = jnp.dot(temb, embedding_weight, preferred_element_type=jnp.float32)
    source = latents.astype(jnp.float32)
    act1 = group_act(source, group_norm_gain[0], group_norm_shift[0])
    hidden1 = (
        block_conv(act1, kernel_weight[0], down_all[:, 0], up_all[:, 0]) + proj[:, None, None, :]
    ).astype(jnp.bfloat16)
    act2 = group_act(hidden1.astype(jnp.float32), group_norm_gain[1], group_norm_shift[1])
    result = source + block_conv(act2, kernel_weight[1], down_all[:, 1], up_all[:, 1])
    return result.astype(jnp.bfloat16)


def solution(mesh):
    in_specs = (
        P("req", "patch", "owner", None),
        P("req", None),
        P(),
        P(),
        P(),
        P(),
        P(("req", "owner"), None, "patch"),
        P(("req", "owner"), None, "patch"),
        P("req", None),
        P(),
    )
    out_specs = P("req", "patch", "owner", None)
    return jax.shard_map(local, mesh=mesh, in_specs=in_specs, out_specs=out_specs, check_vma=False)
```

profile of v0, /device:TPU:1, one launch (start us, length us, event | category | flops | bytes accessed | tf_op | source)
XLA Modules:
  0.0 778.4 jit_solution(10491722644223189108)
XLA Ops:
  6.6 47.2 %all_gather.12 = bf16[1,2,184320]{2,1,0:T(2,128)(2,1)} all-gather(bf16[1,2,5760]{2,1,0:T(2,128)(2,1)} %param.16), channel_id=1, replica_groups=mesh['patch'=32,'req'=4,'owner'=2] {'patch'}, dimensions={2}, use_global_device_ids=true | all-gather | bytes 760320 | tf_op jit(solution)/shard_map/all_gather | solution.py:74
  55.6 135.6 %psum.28 = f32[2,32]{1,0:T(2,128)S(1)} all-reduce(f32[2,32]{1,0:T(2,128)S(1)} %reduce_sum.59), channel_id=1, replica_groups=mesh['patch'=32,'req'=4,'owner'=2] {'patch','owner'}, use_global_device_ids=true, to_apply=%region_2.3 | all-reduce | flops 64 | bytes 512 | tf_op jit(solution)/shard_map/psum | solution.py:26
  192.2 124.0 %psum.29 = f32[2,32]{1,0:T(2,128)S(1)} all-reduce(f32[2,32]{1,0:T(2,128)S(1)} %reduce_sum.62), channel_id=1, replica_groups=mesh['patch'=32,'req'=4,'owner'=2] {'patch','owner'}, use_global_device_ids=true, to_apply=%region_5.6 | all-reduce | flops 64 | bytes 512 | tf_op jit(solution)/shard_map/psum | solution.py:29
  320.5 32.0 %all_gather.14 = bf16[1,2,20480]{2,1,0:T(2,128)(2,1)S(1)} all-gather(bf16[1,2,640]{2,1,0:T(2,128)(2,1)S(1)} %copy-done.16), channel_id=1, replica_groups=mesh['patch'=32,'req'=4,'owner'=2] {'patch'}, dimensions={2}, use_global_device_ids=true | all-gather | bytes 84480 | tf_op jit(solution)/shard_map/all_gather | solution.py:75
  352.5 24.4 %all_gather.15 = bf16[8,2,20480]{2,1,0:T(2,128)(2,1)S(1)} all-gather(bf16[1,2,20480]{2,1,0:T(2,128)(2,1)S(1)} %all_gather.14), channel_id=1, replica_groups=mesh['patch'=32,'req'=4,'owner'=2] {'req','owner'}, dimensions={0}, use_global_device_ids=true | all-gather | bytes 737280 | tf_op jit(solution)/shard_map/all_gather | solution.py:79
  377.0 4.8 slice_bitcast_fusion
  390.1 3.5 collective-permute-start.3
  398.0 5.7 pad_maximum_fusion
  403.7 10.7 %convolution_convert_fusion = bf16[2,2,184320]{2,0,1:T(2,128)(2,1)} fusion(bf16[8,2,184320]{2,1,0:T(2,128)(2,1)} %all-gather.2.cloned.1.call-done, s32[2]{0:T(128)S(1)} %fusion.123), kind=kOutput, calls=%fused_computation | convolution fusion | flops 12533776 | bytes 7372808 | tf_op jit(solution)/shard_map/ik,kjs->ijs/dot_general | solution.py:83
  414.4 4.7 reshape.54
  419.1 3.3 fusion.145
  428.2 2.9 fusion.54
  431.1 2.9 fusion.50
  439.4 2.7 fusion.14
  444.9 9.6 %add_add_fusion.1 = f32[2,8,128,384]{2,3,1,0:T(8,128)} fusion(f32[2,8,128,384]{2,3,1,0:T(8,128)} %fusion.18, f32[2,8,128,384]{2,3,1,0:T(8,128)} %fusion.48, f32[2,8,128,384]{2,3,1,0:T(8,128)} %fusion.50, f32[2,8,128,384]{2,3,1,0:T(8,128)} %fusion.80, f32[2,8,128,384]{2,3,1,0:T(8,128)S(1)} %copy-done.10, f32[2,8,128,384]{2,3,1,0:T(8,128)} %fusion.54, ...), kind=kOutput, calls=%fused_computation.45 | convolution fusion | flops 510590976 | bytes 35520512 | tf_op jit(solution)/shard_map/bhwc,bcd->bhwd/dot_general | solution.py:46
  457.3 122.8 %psum.30 = f32[2,32]{1,0:T(2,128)S(1)} all-reduce(f32[2,32]{1,0:T(2,128)S(1)} %reduce_sum.82), channel_id=1, replica_groups=mesh['patch'=32,'req'=4,'owner'=2] {'patch','owner'}, use_global_device_ids=true, to_apply=%region_9.10 | all-reduce | flops 64 | bytes 512 | tf_op jit(solution)/shard_map/psum | solution.py:26
  581.0 127.5 %psum.31 = f32[2,32]{1,0:T(2,128)S(1)} all-reduce(f32[2,32]{1,0:T(2,128)S(1)} %reduce_sum.85), channel_id=1, replica_groups=mesh['patch'=32,'req'=4,'owner'=2] {'patch','owner'}, use_global_device_ids=true, to_apply=%region_12.13 | all-reduce | flops 64 | bytes 512 | tf_op jit(solution)/shard_map/psum | solution.py:29
  714.9 3.2 fusion.97
  727.7 3.7 collective-permute-start.7
  731.4 4.1 fusion.22
  741.8 5.0 pad_maximum_fusion.1
  752.2 2.9 fusion.40
  755.1 2.9 fusion.36
  760.7 8.9 %add_add_fusion = f32[2,8,128,384]{2,3,1,0:T(8,128)S(1)} fusion(f32[2,8,128,384]{2,3,1,0:T(8,128)} %fusion.26, f32[2,8,128,384]{2,3,1,0:T(8,128)} %fusion.34, f32[2,8,128,384]{2,3,1,0:T(8,128)} %fusion.36, f32[2,8,128,384]{2,3,1,0:T(8,128)S(1)} %copy-done.9, f32[2,8,128,384]{2,3,1,0:T(8,128)} %fusion.38, f32[2,8,128,384]{2,3,1,0:T(8,128)} %fusion.40, ...), kind=kOutput, calls=%fused_computation.44 | convolution fusion | flops 510590976 | bytes 35520512 | tf_op jit(solution)/shard_map/bhwc,bcd->bhwd/dot_general | solution.py:46
  (124 shorter events, 69.0 us)
Async XLA Ops:
  6.5 375.3 %copy-start = (bf16[1280,320]{0,1:T(8,128)(2,1)S(1)}, bf16[1280,320]{0,1:T(8,128)(2,1)}, u32[]{:S(2)}) copy-start(bf16[1280,320]{0,1:T(8,128)(2,1)} %param.12) | copy-start | bytes 2457604
  6.5 184.9 %copy-start.5 = (bf16[2,8,128,320]{2,3,1,0:T(8,128)(2,1)S(1)}, bf16[2,8,128,320]{2,3,1,0:T(8,128)(2,1)}, u32[]{:S(2)}) copy-start(bf16[2,8,128,320]{2,3,1,0:T(8,128)(2,1)} %param.10) | copy-start | bytes 3932164
  6.5 309.9 %copy-start.15 = (f32[2,320]{1,0:T(2,128)S(1)}, f32[2,320]{1,0:T(2,128)}, u32[]{:S(2)}) copy-start(f32[2,320]{1,0:T(2,128)} %param.13) | copy-start | bytes 7684
  6.5 309.9 %copy-start.14 = (f32[2,320]{1,0:T(2,128)S(1)}, f32[2,320]{1,0:T(2,128)}, u32[]{:S(2)}) copy-start(f32[2,320]{1,0:T(2,128)} %param.14) | copy-start | bytes 7684
  6.5 397.2 %all-gather.2.cloned.1.call-start = ((), (), s32[]{:S(2)}) async-start(), calls=%async_computation | async-start | bytes 6635520 | tf_op jit(solution)/shard_map/all_gather | solution.py:78
  53.8 266.6 %copy-start.16 = (bf16[1,2,640]{2,1,0:T(2,128)(2,1)S(1)}, bf16[1,2,640]{2,1,0:T(2,128)(2,1)}, u32[]{:S(2)}) copy-start(bf16[1,2,640]{2,1,0:T(2,128)(2,1)} %param.17) | copy-start | bytes 7684
  317.9 64.4 %collective-permute-start = (bf16[2,1,128,320]{2,3,1,0:T(8,128)(2,1)S(1)}, bf16[2,1,128,320]{2,3,1,0:T(8,128)(2,1)S(1)}, u32[]{:S(2)}, u32[]{:S(2)}) collective-permute-start(bf16[2,1,128,320]{2,3,1,0:T(8,128)(2,1)S(1)} %get-tuple-element.23), channel_id=1, source_target_pairs={{0,8},{8,16},{16,24},{24,32},{32,40},{40,48},{48,56},{56,64},{64,7... | collective-permute-start | bytes 491528 | tf_op jit(solution)/shard_map/ppermute | solution.py:14
  319.2 63.1 %collective-permute-start.1 = (bf16[2,1,128,320]{2,3,1,0:T(8,128)(2,1)S(1)}, bf16[2,1,128,320]{2,3,1,0:T(8,128)(2,1)S(1)}, u32[]{:S(2)}, u32[]{:S(2)}) collective-permute-start(bf16[2,1,128,320]{2,3,1,0:T(8,128)(2,1)S(1)} %get-tuple-element.24), channel_id=1, source_target_pairs={{8,0},{16,8},{24,16},{32,24},{40,32},{48,40},{56,48},{64,56},{72,6... | collective-permute-start | bytes 491528 | tf_op jit(solution)/shard_map/ppermute | solution.py:17
  377.0 5.1 copy-start.17
  377.0 5.1 copy-start.18
  386.9 7.8 collective-permute-start.2
  390.1 6.3 collective-permute-start.3
  708.7 5.5 copy-start.11
  710.1 9.8 %copy-start.3 = (bf16[2,8,128,320]{2,3,1,0:T(8,128)(2,1)}, bf16[2,8,128,320]{2,3,1,0:T(8,128)(2,1)S(1)}, u32[]{:S(2)}) copy-start(bf16[2,8,128,320]{2,3,1,0:T(8,128)(2,1)S(1)} %multiply_convert_fusion) | copy-start | bytes 3932164
  710.2 7.9 %collective-permute-start.4 = (bf16[2,1,128,320]{2,3,1,0:T(8,128)(2,1)S(1)}, bf16[2,1,128,320]{2,3,1,0:T(8,128)(2,1)S(1)}, u32[]{:S(2)}, u32[]{:S(2)}) collective-permute-start(bf16[2,1,128,320]{2,3,1,0:T(8,128)(2,1)S(1)} %get-tuple-element.21), channel_id=1, source_target_pairs={{0,8},{8,16},{16,24},{24,32},{32,40},{40,48},{48,56},{56,64},{64,7... | collective-permute-start | bytes 491528 | tf_op jit(solution)/shard_map/ppermute | solution.py:14
  712.9 7.0 collective-permute-start.5
  724.4 13.8 %collective-permute-start.6 = (bf16[2,10,1,320]{3,0,2,1:T(2,128)(2,1)S(1)}, bf16[2,10,1,320]{3,0,2,1:T(2,128)(2,1)S(1)}, u32[]{:S(2)}, u32[]{:S(2)}) collective-permute-start(bf16[2,10,1,320]{3,0,2,1:T(2,128)(2,1)S(1)} %copy.104), channel_id=1, source_target_pairs={{0,1},{2,3},{4,5},{6,7},{8,9},{10,11},{12,13},{14,15},{16,17},{18,... | collective-permute-start | bytes 38408 | tf_op jit(solution)/shard_map/ppermute | solution.py:14
  725.7 9.8 %slice-start = ((s8[4423680]{0:T(1024)(128)(4,1)}), s8[229376]{0:T(1024)(128)(4,1)S(1)}, s32[]{:S(2)}) async-start(s8[4423680]{0:T(1024)(128)(4,1)} %bitcast.145), calls=%async_computation.1 | async-start | bytes 458752
  727.7 7.8 %slice-start.1 = ((s8[4423680]{0:T(1024)(128)(4,1)}), s8[4194304]{0:T(1024)(128)(4,1)S(1)}, s32[]{:S(2)}) async-start(s8[4423680]{0:T(1024)(128)(4,1)} %bitcast.145), calls=%async_computation.2 | async-start | bytes 8388608
  727.7 7.8 %copy-start.4 = (bf16[2,8,128,320]{2,3,1,0:T(8,128)(2,1)S(1)}, bf16[2,8,128,320]{2,3,1,0:T(8,128)(2,1)}, u32[]{:S(2)}) copy-start(bf16[2,8,128,320]{2,3,1,0:T(8,128)(2,1)} %copy-done.3) | copy-start | bytes 3932164
  727.7 12.5 %collective-permute-start.7 = (bf16[2,10,1,320]{3,0,2,1:T(2,128)(2,1)S(1)}, bf16[2,10,1,320]{3,0,2,1:T(2,128)(2,1)S(1)}, u32[]{:S(2)}, u32[]{:S(2)}) collective-permute-start(bf16[2,10,1,320]{3,0,2,1:T(2,128)(2,1)S(1)} %copy.109), channel_id=1, source_target_pairs={{1,0},{3,2},{5,4},{7,6},{9,8},{11,10},{13,12},{15,14},{17,16},{19,... | collective-permute-start | bytes 38408 | tf_op jit(solution)/shard_map/ppermute | solution.py:17
  740.1 6.7 slice-start.2
  760.7 8.9 %copy-start.6 = (bf16[2,8,128,320]{2,3,1,0:T(8,128)(2,1)S(1)}, bf16[2,8,128,320]{2,3,1,0:T(8,128)(2,1)}, u32[]{:S(2)}) copy-start(bf16[2,8,128,320]{2,3,1,0:T(8,128)(2,1)} %param.10) | copy-start | bytes 3932164
  760.7 10.6 %copy-start.1 = (bf16[1280,320]{0,1:T(8,128)(2,1)S(1)}, bf16[1280,320]{0,1:T(8,128)(2,1)}, u32[]{:S(2)}) copy-start(bf16[1280,320]{0,1:T(8,128)(2,1)} %param.12) | copy-start | bytes 2457604
  (8 other events, 26.5 us)
Sparse Core Ops, SparseCore 0:
  54.0 51.1 all-gather.1
where the time goes:
time: 784 us; the launch traced here: 778 us
  blocking collectives  614 us (78%)
  matrix products  79 us (10%)
  local copies, waits for them, and re-layouts  37.7 us (5%)
  other arithmetic  17 us (2%)
  starting transfers between devices  15 us (2%)
  between operations  14.1 us (2%)
    psum x2, blocking collectives, group_act(): total = lax.psum(jnp.sum(grouped, axis=(1, 2, 4)), ('patch', 'owner'))  258 us
    psum x2, blocking collectives, group_act(): lax.psum(jnp.sum(centered * centered, axis=(1, 2, 4)), ('patch', 'owner'))  252 us
    dot_general x18, matrix products, block_conv(): jnp.einsum('bhwc,bcd->bhwd', window, joined[:, tap], preferred_element_ty...  62.9 us
    all_gather x1, blocking collectives, local(): lax.all_gather(plugin_reduce_library, 'patch', axis=2, tiled=True)  47.2 us
    all_gather x1, blocking collectives, local(): lax.all_gather(plugin_expand_library, 'patch', axis=2, tiled=True)  32 us
    all_gather x1, blocking collectives, local(): lax.all_gather(full_up, ('req', 'owner'), axis=0, tiled=True)  24.4 us
  transfers between devices with their start and end apart: 9, of which 1 were waited for; matrix products, arithmetic and copies ran while one was open for 5% of the time, Pallas kernels for 0%

commit v1 on v0

--- a/solution.py
+++ b/solution.py
@@ -23,7 +23,7 @@
     images, rows, columns, chans = values.shape
     grouped = values.reshape(images, rows, columns, GROUPS, chans // GROUPS)
     count = rows * columns * (chans // GROUPS) * lax.axis_size("patch") * lax.axis_size("owner")
-    total = lax.psum(jnp.sum(grouped, axis=(1, 2, 4)), ("patch", "owner"))
+    total = jnp.sum(lax.all_gather(jnp.sum(grouped, axis=(1, 2, 4)), ("patch", "owner")), axis=0)
     mean = total / count
     centered = grouped - mean[:, None, None, :, None]
     spread = lax.psum(jnp.sum(centered * centered, axis=(1, 2, 4)), ("patch", "owner"))

time: 784 us -> 622 us (0.79)
  blocking collectives: 614 us -> 449 us
    psum x2 -> x0, blocking collectives: 258 us -> none  [group_act(): total = lax.psum(jnp.sum(grouped, axis=(1, 2, 4)), ('patch', 'owner'))]
    all_gather x0 -> x2, blocking collectives: none -> 95.2 us  [group_act(): lax.all_gather(jnp.sum(grouped, axis=(1, 2, 4)), ('patch', 'owner'))]
  transfers between devices with their start and end apart: 9 -> 9, of which waited for: 1 -> 1; matrix products, arithmetic and copies ran while one was open for 5% -> 7% of each run, Pallas kernels for 0% -> 0%
where the time goes in v1:
time: 622 us; the launch traced here: 615 us
  blocking collectives  449 us (72%)
  matrix products  79 us (13%)
  local copies, waits for them, and re-layouts  37.4 us (6%)
  starting transfers between devices  18 us (3%)
  other arithmetic  17.2 us (3%)
  between operations  14.1 us (2%)
    psum x2, blocking collectives, group_act(): lax.psum(jnp.sum(centered * centered, axis=(1, 2, 4)), ('patch', 'owner'))  247 us
    all_gather x2, blocking collectives, group_act(): lax.all_gather(jnp.sum(grouped, axis=(1, 2, 4)), ('patch', 'owner'))  95.2 us
    dot_general x18, matrix products, block_conv(): jnp.einsum('bhwc,bcd->bhwd', window, joined[:, tap], preferred_element_ty...  62.9 us
    all_gather x1, blocking collectives, local(): lax.all_gather(plugin_reduce_library, 'patch', axis=2, tiled=True)  47.2 us
    all_gather x1, blocking collectives, local(): lax.all_gather(plugin_expand_library, 'patch', axis=2, tiled=True)  32.6 us
    all_gather x1, blocking collectives, local(): lax.all_gather(full_up, ('req', 'owner'), axis=0, tiled=True)  26.5 us
    ppermute x4, starting transfers between devices, padded_2(): lax.ppermute(lax.slice_in_dim(block, 0, width, axis=dim), axis, backward)  12.8 us
  transfers between devices with their start and end apart: 9, of which 1 were waited for; matrix products, arithmetic and copies ran while one was open for 7% of the time, Pallas kernels for 0%

profile of v1, /device:TPU:1, one launch (start us, length us, event | category | flops | bytes accessed | tf_op | source)
XLA Modules:
  0.0 615.5 jit_solution(13456152339179434330)
XLA Ops:
  6.6 47.2 %all_gather.26 = bf16[1,2,184320]{2,1,0:T(2,128)(2,1)} all-gather(bf16[1,2,5760]{2,1,0:T(2,128)(2,1)} %param.16), channel_id=1, replica_groups=mesh['patch'=32,'req'=4,'owner'=2] {'patch'}, dimensions={2}, use_global_device_ids=true | all-gather | bytes 760320 | tf_op jit(solution)/shard_map/all_gather | solution.py:74
  55.6 54.5 %all-gather.2 = f32[64,2,32]{2,1,0:T(2,128)S(1)} all-gather(f32[1,2,32]{2,1,0:T(2,128)S(1)} %bitcast.169), channel_id=2, replica_groups=mesh['patch'=32,'req'=4,'owner'=2] {'patch','owner'}, dimensions={0}, use_global_device_ids=true | all-gather | bytes 16640 | tf_op jit(solution)/shard_map/all_gather | solution.py:26
  111.1 123.6 %psum.14 = f32[2,32]{1,0:T(2,128)S(1)} all-reduce(f32[2,32]{1,0:T(2,128)S(1)} %reduce_sum.97), channel_id=1, replica_groups=mesh['patch'=32,'req'=4,'owner'=2] {'patch','owner'}, use_global_device_ids=true, to_apply=%region_5.6 | all-reduce | flops 64 | bytes 512 | tf_op jit(solution)/shard_map/psum | solution.py:29
  239.0 32.6 %all_gather.28 = bf16[1,2,20480]{2,1,0:T(2,128)(2,1)S(1)} all-gather(bf16[1,2,640]{2,1,0:T(2,128)(2,1)S(1)} %copy-done.16), channel_id=1, replica_groups=mesh['patch'=32,'req'=4,'owner'=2] {'patch'}, dimensions={2}, use_global_device_ids=true | all-gather | bytes 84480 | tf_op jit(solution)/shard_map/all_gather | solution.py:75
  271.6 26.5 %all_gather.29 = bf16[8,2,20480]{2,1,0:T(2,128)(2,1)S(1)} all-gather(bf16[1,2,20480]{2,1,0:T(2,128)(2,1)S(1)} %all_gather.28), channel_id=1, replica_groups=mesh['patch'=32,'req'=4,'owner'=2] {'req','owner'}, dimensions={0}, use_global_device_ids=true | all-gather | bytes 737280 | tf_op jit(solution)/shard_map/all_gather | solution.py:79
  298.1 4.8 slice_bitcast_fusion
  311.2 3.5 collective-permute-start.3
  319.1 5.7 pad_maximum_fusion
  324.8 10.7 %convolution_convert_fusion = bf16[2,2,184320]{2,0,1:T(2,128)(2,1)} fusion(bf16[8,2,184320]{2,1,0:T(2,128)(2,1)} %all-gather.6.cloned.1.call-done, s32[2]{0:T(128)S(1)} %fusion.123), kind=kOutput, calls=%fused_computation | convolution fusion | flops 12533776 | bytes 7372808 | tf_op jit(solution)/shard_map/ik,kjs->ijs/dot_general | solution.py:83
  335.5 4.7 reshape.66
  340.2 3.3 fusion.145
  349.3 2.9 fusion.54
  352.2 2.9 fusion.50
  360.5 2.7 fusion.14
  366.0 9.6 %add_add_fusion.1 = f32[2,8,128,384]{2,3,1,0:T(8,128)} fusion(f32[2,8,128,384]{2,3,1,0:T(8,128)} %fusion.18, f32[2,8,128,384]{2,3,1,0:T(8,128)} %fusion.48, f32[2,8,128,384]{2,3,1,0:T(8,128)} %fusion.50, f32[2,8,128,384]{2,3,1,0:T(8,128)} %fusion.80, f32[2,8,128,384]{2,3,1,0:T(8,128)S(1)} %copy-done.10, f32[2,8,128,384]{2,3,1,0:T(8,128)} %fusion.54, ...), kind=kOutput, calls=%fused_computation.45 | convolution fusion | flops 510590976 | bytes 35520512 | tf_op jit(solution)/shard_map/bhwc,bcd->bhwd/dot_general | solution.py:46
  378.4 40.6 %all-gather.3 = f32[64,2,32]{2,1,0:T(2,128)S(1)} all-gather(f32[1,2,32]{2,1,0:T(2,128)S(1)} %bitcast.170), channel_id=3, replica_groups=mesh['patch'=32,'req'=4,'owner'=2] {'patch','owner'}, dimensions={0}, use_global_device_ids=true | all-gather | bytes 16640 | tf_op jit(solution)/shard_map/all_gather | solution.py:26
  420.1 123.8 %psum.15 = f32[2,32]{1,0:T(2,128)S(1)} all-reduce(f32[2,32]{1,0:T(2,128)S(1)} %reduce_sum.105), channel_id=1, replica_groups=mesh['patch'=32,'req'=4,'owner'=2] {'patch','owner'}, use_global_device_ids=true, to_apply=%region_12.13 | all-reduce | flops 64 | bytes 512 | tf_op jit(solution)/shard_map/psum | solution.py:29
  550.1 3.2 fusion.97
  562.1 6.7 %collective-permute-start.7 = (bf16[2,10,1,320]{3,0,2,1:T(2,128)(2,1)S(1)}, bf16[2,10,1,320]{3,0,2,1:T(2,128)(2,1)S(1)}, u32[]{:S(2)}, u32[]{:S(2)}) collective-permute-start(bf16[2,10,1,320]{3,0,2,1:T(2,128)(2,1)S(1)} %copy.109), channel_id=1, source_target_pairs={{1,0},{3,2},{5,4},{7,6},{9,8},{11,10},{13,12},{15,14},{17,16},{19,... | collective-permute-start | bytes 38408 | tf_op jit(solution)/shard_map/ppermute | solution.py:17
  568.8 4.1 fusion.22
  578.9 5.0 pad_maximum_fusion.1
  589.4 2.9 fusion.40
  592.3 2.9 fusion.36
  597.8 8.9 %add_add_fusion = f32[2,8,128,384]{2,3,1,0:T(8,128)S(1)} fusion(f32[2,8,128,384]{2,3,1,0:T(8,128)} %fusion.26, f32[2,8,128,384]{2,3,1,0:T(8,128)} %fusion.34, f32[2,8,128,384]{2,3,1,0:T(8,128)} %fusion.36, f32[2,8,128,384]{2,3,1,0:T(8,128)S(1)} %copy-done.9, f32[2,8,128,384]{2,3,1,0:T(8,128)} %fusion.38, f32[2,8,128,384]{2,3,1,0:T(8,128)} %fusion.40, ...), kind=kOutput, calls=%fused_computation.44 | convolution fusion | flops 510590976 | bytes 35520512 | tf_op jit(solution)/shard_map/bhwc,bcd->bhwd/dot_general | solution.py:46
  (126 shorter events, 68.0 us)
Async XLA Ops:
  6.5 296.3 %copy-start = (bf16[1280,320]{0,1:T(8,128)(2,1)S(1)}, bf16[1280,320]{0,1:T(8,128)(2,1)}, u32[]{:S(2)}) copy-start(bf16[1280,320]{0,1:T(8,128)(2,1)} %param.12) | copy-start | bytes 2457604
  6.5 103.9 %copy-start.5 = (bf16[2,8,128,320]{2,3,1,0:T(8,128)(2,1)S(1)}, bf16[2,8,128,320]{2,3,1,0:T(8,128)(2,1)}, u32[]{:S(2)}) copy-start(bf16[2,8,128,320]{2,3,1,0:T(8,128)(2,1)} %param.10) | copy-start | bytes 3932164
  6.5 228.4 %copy-start.15 = (f32[2,320]{1,0:T(2,128)S(1)}, f32[2,320]{1,0:T(2,128)}, u32[]{:S(2)}) copy-start(f32[2,320]{1,0:T(2,128)} %param.13) | copy-start | bytes 7684
  6.5 228.4 %copy-start.14 = (f32[2,320]{1,0:T(2,128)S(1)}, f32[2,320]{1,0:T(2,128)}, u32[]{:S(2)}) copy-start(f32[2,320]{1,0:T(2,128)} %param.14) | copy-start | bytes 7684
  6.5 318.3 %all-gather.6.cloned.1.call-start = ((), (), s32[]{:S(2)}) async-start(), calls=%async_computation | async-start | bytes 6635520 | tf_op jit(solution)/shard_map/all_gather | solution.py:78
  53.8 185.1 %copy-start.16 = (bf16[1,2,640]{2,1,0:T(2,128)(2,1)S(1)}, bf16[1,2,640]{2,1,0:T(2,128)(2,1)}, u32[]{:S(2)}) copy-start(bf16[1,2,640]{2,1,0:T(2,128)(2,1)} %param.17) | copy-start | bytes 7684
  236.4 67.0 %collective-permute-start = (bf16[2,1,128,320]{2,3,1,0:T(8,128)(2,1)S(1)}, bf16[2,1,128,320]{2,3,1,0:T(8,128)(2,1)S(1)}, u32[]{:S(2)}, u32[]{:S(2)}) collective-permute-start(bf16[2,1,128,320]{2,3,1,0:T(8,128)(2,1)S(1)} %get-tuple-element.23), channel_id=1, source_target_pairs={{0,8},{8,16},{16,24},{24,32},{32,40},{40,48},{48,56},{56,64},{64,7... | collective-permute-start | bytes 491528 | tf_op jit(solution)/shard_map/ppermute | solution.py:14
  237.7 65.7 %collective-permute-start.1 = (bf16[2,1,128,320]{2,3,1,0:T(8,128)(2,1)S(1)}, bf16[2,1,128,320]{2,3,1,0:T(8,128)(2,1)S(1)}, u32[]{:S(2)}, u32[]{:S(2)}) collective-permute-start(bf16[2,1,128,320]{2,3,1,0:T(8,128)(2,1)S(1)} %get-tuple-element.24), channel_id=1, source_target_pairs={{8,0},{16,8},{24,16},{32,24},{40,32},{48,40},{56,48},{64,56},{72,6... | collective-permute-start | bytes 491528 | tf_op jit(solution)/shard_map/ppermute | solution.py:17
  298.1 5.1 copy-start.17
  298.1 5.1 copy-start.18
  308.0 7.8 %collective-permute-start.2 = (bf16[2,10,1,320]{3,0,2,1:T(2,128)(2,1)S(1)}, bf16[2,10,1,320]{3,0,2,1:T(2,128)(2,1)S(1)}, u32[]{:S(2)}, u32[]{:S(2)}) collective-permute-start(bf16[2,10,1,320]{3,0,2,1:T(2,128)(2,1)S(1)} %copy.87), channel_id=1, source_target_pairs={{0,1},{2,3},{4,5},{6,7},{8,9},{10,11},{12,13},{14,15},{16,17},{18,... | collective-permute-start | bytes 38408 | tf_op jit(solution)/shard_map/ppermute | solution.py:14
  311.2 6.3 %collective-permute-start.3 = (bf16[2,10,1,320]{3,0,2,1:T(2,128)(2,1)S(1)}, bf16[2,10,1,320]{3,0,2,1:T(2,128)(2,1)S(1)}, u32[]{:S(2)}, u32[]{:S(2)}) collective-permute-start(bf16[2,10,1,320]{3,0,2,1:T(2,128)(2,1)S(1)} %copy.94), channel_id=1, source_target_pairs={{1,0},{3,2},{5,4},{7,6},{9,8},{11,10},{13,12},{15,14},{17,16},{19,... | collective-permute-start | bytes 38408 | tf_op jit(solution)/shard_map/ppermute | solution.py:17
  544.0 5.5 copy-start.11
  545.4 8.9 %copy-start.3 = (bf16[2,8,128,320]{2,3,1,0:T(8,128)(2,1)}, bf16[2,8,128,320]{2,3,1,0:T(8,128)(2,1)S(1)}, u32[]{:S(2)}) copy-start(bf16[2,8,128,320]{2,3,1,0:T(8,128)(2,1)S(1)} %multiply_convert_fusion) | copy-start | bytes 3932164
  545.5 7.9 %collective-permute-start.4 = (bf16[2,1,128,320]{2,3,1,0:T(8,128)(2,1)S(1)}, bf16[2,1,128,320]{2,3,1,0:T(8,128)(2,1)S(1)}, u32[]{:S(2)}, u32[]{:S(2)}) collective-permute-start(bf16[2,1,128,320]{2,3,1,0:T(8,128)(2,1)S(1)} %get-tuple-element.21), channel_id=1, source_target_pairs={{0,8},{8,16},{16,24},{24,32},{32,40},{40,48},{48,56},{56,64},{64,7... | collective-permute-start | bytes 491528 | tf_op jit(solution)/shard_map/ppermute | solution.py:14
  548.2 6.1 collective-permute-start.5
  558.8 16.8 %collective-permute-start.6 = (bf16[2,10,1,320]{3,0,2,1:T(2,128)(2,1)S(1)}, bf16[2,10,1,320]{3,0,2,1:T(2,128)(2,1)S(1)}, u32[]{:S(2)}, u32[]{:S(2)}) collective-permute-start(bf16[2,10,1,320]{3,0,2,1:T(2,128)(2,1)S(1)} %copy.104), channel_id=1, source_target_pairs={{0,1},{2,3},{4,5},{6,7},{8,9},{10,11},{12,13},{14,15},{16,17},{18,... | collective-permute-start | bytes 38408 | tf_op jit(solution)/shard_map/ppermute | solution.py:14
  560.1 12.8 %slice-start = ((s8[4423680]{0:T(1024)(128)(4,1)}), s8[229376]{0:T(1024)(128)(4,1)S(1)}, s32[]{:S(2)}) async-start(s8[4423680]{0:T(1024)(128)(4,1)} %bitcast.147), calls=%async_computation.1 | async-start | bytes 458752
  562.0 10.8 %slice-start.1 = ((s8[4423680]{0:T(1024)(128)(4,1)}), s8[4194304]{0:T(1024)(128)(4,1)S(1)}, s32[]{:S(2)}) async-start(s8[4423680]{0:T(1024)(128)(4,1)} %bitcast.147), calls=%async_computation.2 | async-start | bytes 8388608
  562.0 10.8 %copy-start.4 = (bf16[2,8,128,320]{2,3,1,0:T(8,128)(2,1)S(1)}, bf16[2,8,128,320]{2,3,1,0:T(8,128)(2,1)}, u32[]{:S(2)}) copy-start(bf16[2,8,128,320]{2,3,1,0:T(8,128)(2,1)} %copy-done.3) | copy-start | bytes 3932164
  562.1 15.2 %collective-permute-start.7 = (bf16[2,10,1,320]{3,0,2,1:T(2,128)(2,1)S(1)}, bf16[2,10,1,320]{3,0,2,1:T(2,128)(2,1)S(1)}, u32[]{:S(2)}, u32[]{:S(2)}) collective-permute-start(bf16[2,10,1,320]{3,0,2,1:T(2,128)(2,1)S(1)} %copy.109), channel_id=1, source_target_pairs={{1,0},{3,2},{5,4},{7,6},{9,8},{11,10},{13,12},{15,14},{17,16},{19,... | collective-permute-start | bytes 38408 | tf_op jit(solution)/shard_map/ppermute | solution.py:17
  577.3 6.7 %slice-start.2 = ((s8[4423680]{0:T(1024)(128)(4,1)}), s8[229376]{0:T(1024)(128)(4,1)S(1)}, s32[]{:S(2)}) async-start(s8[4423680]{0:T(1024)(128)(4,1)} %bitcast.149), calls=%async_computation.3 | async-start | bytes 458752
  597.8 8.9 %copy-start.6 = (bf16[2,8,128,320]{2,3,1,0:T(8,128)(2,1)S(1)}, bf16[2,8,128,320]{2,3,1,0:T(8,128)(2,1)}, u32[]{:S(2)}) copy-start(bf16[2,8,128,320]{2,3,1,0:T(8,128)(2,1)} %param.10) | copy-start | bytes 3932164
  597.8 10.6 %copy-start.1 = (bf16[1280,320]{0,1:T(8,128)(2,1)S(1)}, bf16[1280,320]{0,1:T(8,128)(2,1)}, u32[]{:S(2)}) copy-start(bf16[1280,320]{0,1:T(8,128)(2,1)} %param.12) | copy-start | bytes 2457604
  (8 other events, 26.5 us)
Sparse Core Ops, SparseCore 0:
  54.0 51.1 all-gather.5
